TPU v7x, 32 devices: a whole 2x2x4 slice. The times are simulated.
32 devices in a mesh: ma: 16 (over z, y, core), freq: 2 (over x).
Axes of the slice: x: 2, y: 2, z: 4, core: 2. Of those that a mesh axis runs over, the one named last changes fastest.
Arguments:
- right_side: float32 [128, 8, 2, 512], P('ma', 'freq'), may hold values from -60 to 60
- start_field: float32 [128, 8, 2, 512], P('ma', 'freq'), may hold values from -6 to 6
- beam: float32 [128, 8, 2, 16, 512], P('ma', 'freq'), may hold values from -0.75 to 0.75
- noise: float32 [128, 8, 16], P('ma', 'freq'), may hold values from 0.3 to 3
- inv_power: float32 [512], replicated, may hold values from 0.5 to 2
- smooth: float32 [512], replicated, may hold values from 0.5 to 4
Outputs:
- solution_field: float32 [128, 8, 2, 512], P('ma', 'freq')
- residual: float32 [128, 8, 2, 512], P('ma', 'freq')
All inputs are finite; a program needn't handle non-finite values.
Results may differ from a plain program's by a relative error of at most 0.0003.
Values sent between devices are 32-bit elements; how exact they have to be, the bound alone decides.
A program may use at most 64 MiB of HBM per device.

v0:
```python
import jax
import jax.numpy as jnp
from jax import lax
from jax.sharding import PartitionSpec as P

ITERS = 2


def extended(array, sides, width):
    for axis, dim in sides:
        size, length = (lax.axis_size(axis), array.shape[dim])
        up = [(i, (i + 1) % size) for i in range(size - 1)]
        down = [(j, i) for i, j in up]
        last = lax.slice_in_dim(array, length - width, length, axis=dim)
        leading = lax.slice_in_dim(array, 0, width, axis=dim)
        before = lax.ppermute(last, axis, up)
        after = lax.ppermute(leading, axis, down)
        array = jnp.concatenate([before, array, after], axis=dim)
    return array


def beam_image(field, beam, noise):
    projected = jnp.einsum("mfakl,mfbl->mfabk", beam, field, precision=lax.Precision.HIGHEST)
    real_part = projected[:, :, 0, 0] + projected[:, :, 1, 1]
    imaginary = projected[:, :, 0, 1] - projected[:, :, 1, 0]
    weighted = jnp.stack([real_part, imaginary], axis=2) * noise[:, :, None, :]
    back = jnp.einsum("mfakl,mfbk->mfabl", beam, weighted, precision=lax.Precision.HIGHEST)
    return jnp.stack(
        [back[:, :, 0, 0] - back[:, :, 1, 1], back[:, :, 0, 1] + back[:, :, 1, 0]], axis=2
    )


def prior_term(padded, field, first, total, smooth):
    channel = first + jnp.arange(field.shape[1], dtype=jnp.int32)
    weight = (channel > 0).astype(jnp.float32) + (channel < total - 1).astype(jnp.float32)
    return smooth * (weight[None, :, None, None] * field - padded[:, :-2] - padded[:, 2:])


def two_products(vector, applied):
    return lax.psum((jnp.sum(vector * vector), jnp.sum(vector * applied)), ("ma", "freq"))


def shards(right_side, start_field, beam, noise, inv_power, smooth):
    first = lax.axis_index("freq") * right_side.shape[1]
    total = right_side.shape[1] * lax.axis_size("freq")

    def padded_of(field):
        return extended(field, (("freq", 1),), 1)

    def operate(field):
        prior = prior_term(padded_of(field), field, first, total, smooth)
        return beam_image(field, beam, noise) + inv_power * field + prior

    solution = start_field
    resid_now = right_side - operate(start_field)
    applied = operate(resid_now)
    norm_now, curve_now = two_products(resid_now, applied)
    step_size = norm_now / curve_now
    direction = resid_now
    along = applied
    for turn in range(ITERS):
        solution = solution + step_size * direction
        resid_now = resid_now - step_size * along
        if turn + 1 < ITERS:
            applied = operate(resid_now)
            norm_next, curve_now = two_products(resid_now, applied)
            growth = norm_next / norm_now
            step_size = norm_next / (curve_now - growth * norm_next / step_size)
            direction = resid_now + growth * direction
            along = applied + growth * along
            norm_now = norm_next
    return (solution, resid_now)


def solution(mesh):
    in_specs = (
        P("ma", "freq", None, None),
        P("ma", "freq", None, None),
        P("ma", "freq", None, None, None),
        P("ma", "freq", None),
        P(),
        P(),
    )
    out_specs = (P("ma", "freq", None, None), P("ma", "freq", None, None))
    return jax.shard_map(shards, mesh=mesh, in_specs=in_specs, out_specs=out_specs, check_vma=False)
```

profile of v0, /device:TPU:0, one launch (start us, length us, event | category | flops | bytes accessed | tf_op | source)
XLA Modules:
  0.0 144.0 jit_solution(10948142598104500641)
XLA Ops:
  0.7 0.9 fusion.42
  1.6 4.9 %collective-permute-start = (f32[8,1,2,512]{3,2,1,0:T(2,128)S(1)}, f32[8,1,2,512]{3,2,1,0:T(2,128)S(1)}, u32[]{:S(2)}, u32[]{:S(2)}) collective-permute-start(f32[8,1,2,512]{3,2,1,0:T(2,128)S(1)} %get-tuple-element.22), channel_id=1, source_target_pairs={{0,1},{2,3},{4,5},{6,7},{8,9},{10,11},{12,13},{14,15},{16,17},{18,... | collective-permute-start | bytes 98312 | tf_op jit(solution)/shard_map/ppermute | solution.py:16
  6.5 1.3 collective-permute-start.1
  7.8 8.3 %convolution_bitcast_fusion.1 = f32[8,4,2,2,16]{4,3,2,1,0:T(2,128)S(1)} fusion(f32[8,4,2,16,512]{4,3,2,1,0:T(8,128)S(1)} %copy-done, f32[8,4,2,512]{3,2,1,0:T(2,128)} %param.7), kind=kOutput, calls=%fused_computation.1 | convolution fusion | flops 12582912 | bytes 2236416 | tf_op jit(solution)/shard_map/mfakl,mfbl->mfabk/dot_general | solution.py:23
  16.2 1.1 convolution_bitcast_fusion
  17.6 0.3 fusion.11
  17.9 7.4 %fusion.15 = f32[8,4,2,2,16]{4,2,3,1,0:T(2,128)S(1)} fusion(f32[8,4,2,16,512]{4,3,2,1,0:T(8,128)S(1)} %copy-done, f32[8,4,2,512]{3,2,1,0:T(2,128)S(1)} %fusion.11), kind=kOutput, calls=%fused_computation.28 | convolution fusion | flops 12582912 | bytes 2236416 | tf_op jit(solution)/shard_map/mfakl,mfbl->mfabk/dot_general | solution.py:23
  25.4 1.3 fusion.30
  26.7 0.1 copy.46
  26.9 4.5 %collective-permute-start.2 = (f32[8,1,2,512]{3,2,1,0:T(2,128)S(1)}, f32[8,1,2,512]{3,2,1,0:T(2,128)S(1)}, u32[]{:S(2)}, u32[]{:S(2)}) collective-permute-start(f32[8,1,2,512]{3,2,1,0:T(2,128)S(1)} %get-tuple-element.20), channel_id=1, source_target_pairs={{0,1},{2,3},{4,5},{6,7},{8,9},{10,11},{12,13},{14,15},{16,17},{18,... | collective-permute-start | bytes 98312 | tf_op jit(solution)/shard_map/ppermute | solution.py:16
  31.4 1.3 collective-permute-start.3
  32.7 0.1 fusion.21
  33.0 4.2 %collective-permute-done.3 = f32[8,1,2,512]{3,2,1,0:T(2,128)S(1)} collective-permute-done((f32[8,1,2,512]{3,2,1,0:T(2,128)S(1)}, f32[8,1,2,512]{3,2,1,0:T(2,128)S(1)}, u32[]{:S(2)}, u32[]{:S(2)}) %collective-permute-start.3) | collective-permute-done | bytes 32800 | tf_op jit(solution)/shard_map/ppermute | solution.py:17
  37.2 1.1 multiply_reduce_fusion.2
  38.3 39.8 %all-reduce.1 = (f32[]{:T(128)}, f32[]{:T(128)}) all-reduce(f32[]{:T(128)} %get-tuple-element.5, f32[]{:T(128)} %get-tuple-element.4), channel_id=1, replica_groups=mesh['ma'=16,'freq'=2] {'ma','freq'}, use_global_device_ids=true, to_apply=%region_1.0 | all-reduce | flops 2 | bytes 16 | tf_op jit(solution)/shard_map/psum | solution.py:40
  79.4 7.4 %fusion.13 = f32[8,4,2,2,16]{4,2,3,1,0:T(2,128)S(1)} fusion(f32[8,4,2,16,512]{4,3,2,1,0:T(8,128)S(1)} %copy-done, f32[8,4,2,512]{3,2,1,0:T(2,128)S(1)} %bitcast.90), kind=kOutput, calls=%fused_computation.26 | convolution fusion | flops 12582912 | bytes 2236416 | tf_op jit(solution)/shard_map/mfakl,mfbl->mfabk/dot_general | solution.py:23
  86.9 1.1 fusion.28
  88.2 4.2 %collective-permute-start.4 = (f32[8,1,2,512]{3,2,1,0:T(2,128)S(1)}, f32[8,1,2,512]{3,2,1,0:T(2,128)S(1)}, u32[]{:S(2)}, u32[]{:S(2)}) collective-permute-start(f32[8,1,2,512]{3,2,1,0:T(2,128)S(1)} %get-tuple-element.18), channel_id=1, source_target_pairs={{0,1},{2,3},{4,5},{6,7},{8,9},{10,11},{12,13},{14,15},{16,17},{18,... | collective-permute-start | bytes 98312 | tf_op jit(solution)/shard_map/ppermute | solution.py:16
  92.4 1.3 collective-permute-start.5
  93.7 0.1 fusion.19
  93.9 4.2 %collective-permute-done.5 = f32[8,1,2,512]{3,2,1,0:T(2,128)S(1)} collective-permute-done((f32[8,1,2,512]{3,2,1,0:T(2,128)S(1)}, f32[8,1,2,512]{3,2,1,0:T(2,128)S(1)}, u32[]{:S(2)}, u32[]{:S(2)}) %collective-permute-start.5) | collective-permute-done | bytes 32800 | tf_op jit(solution)/shard_map/ppermute | solution.py:17
  98.2 1.1 multiply_reduce_fusion
  99.3 39.4 %all-reduce = (f32[]{:T(128)}, f32[]{:T(128)}) all-reduce(f32[]{:T(128)} %get-tuple-element.3, f32[]{:T(128)} %get-tuple-element.2), channel_id=1, replica_groups=mesh['ma'=16,'freq'=2] {'ma','freq'}, use_global_device_ids=true, to_apply=%region_5.0 | all-reduce | flops 2 | bytes 16 | tf_op jit(solution)/shard_map/psum | solution.py:40
  143.3 0.8 multiply_subtract_fusion
  (32 shorter events, 0.8 us)
Async XLA Ops:
  0.6 7.1 %copy-start = (f32[8,4,2,16,512]{4,3,2,1,0:T(8,128)S(1)}, f32[8,4,2,16,512]{4,3,2,1,0:T(8,128)}, u32[]{:S(2)}) copy-start(f32[8,4,2,16,512]{4,3,2,1,0:T(8,128)} %param.8) | copy-start | bytes 6291460
  0.6 15.5 %copy-start.2 = (f32[8,4,16]{2,1,0:T(4,128)S(1)}, f32[8,4,16]{2,1,0:T(4,128)}, u32[]{:S(2)}) copy-start(f32[8,4,16]{2,1,0:T(4,128)} %param.9) | copy-start | bytes 6148
  1.6 16.0 %collective-permute-start = (f32[8,1,2,512]{3,2,1,0:T(2,128)S(1)}, f32[8,1,2,512]{3,2,1,0:T(2,128)S(1)}, u32[]{:S(2)}, u32[]{:S(2)}) collective-permute-start(f32[8,1,2,512]{3,2,1,0:T(2,128)S(1)} %get-tuple-element.22), channel_id=1, source_target_pairs={{0,1},{2,3},{4,5},{6,7},{8,9},{10,11},{12,13},{14,15},{16,17},{18,... | collective-permute-start | bytes 98312 | tf_op jit(solution)/shard_map/ppermute | solution.py:16
  6.5 11.1 %collective-permute-start.1 = (f32[8,1,2,512]{3,2,1,0:T(2,128)S(1)}, f32[8,1,2,512]{3,2,1,0:T(2,128)S(1)}, u32[]{:S(2)}, u32[]{:S(2)}) collective-permute-start(f32[8,1,2,512]{3,2,1,0:T(2,128)S(1)} %get-tuple-element.23), channel_id=1, source_target_pairs={{1,0},{3,2},{5,4},{7,6},{9,8},{11,10},{13,12},{15,14},{17,16},{19,... | collective-permute-start | bytes 98312 | tf_op jit(solution)/shard_map/ppermute | solution.py:17
  16.1 1.5 %copy-start.1 = (f32[8,4,2,512]{3,2,1,0:T(2,128)S(1)}, f32[8,4,2,512]{3,2,1,0:T(2,128)}, u32[]{:S(2)}) copy-start(f32[8,4,2,512]{3,2,1,0:T(2,128)} %param.7) | copy-start | bytes 393220
  16.1 1.5 %copy-start.3 = (f32[8,4,2,512]{3,2,1,0:T(2,128)S(1)}, f32[8,4,2,512]{3,2,1,0:T(2,128)}, u32[]{:S(2)}) copy-start(f32[8,4,2,512]{3,2,1,0:T(2,128)} %param.6) | copy-start | bytes 393220
  16.1 1.6 %copy-start.4 = (f32[512]{0:T(512)S(1)}, f32[512]{0:T(512)}, u32[]{:S(2)}) copy-start(f32[512]{0:T(512)} %param.11) | copy-start | bytes 6148
  16.1 1.5 %copy-start.5 = (f32[512]{0:T(512)S(1)}, f32[512]{0:T(512)}, u32[]{:S(2)}) copy-start(f32[512]{0:T(512)} %param.10) | copy-start | bytes 6148
  26.9 6.1 %collective-permute-start.2 = (f32[8,1,2,512]{3,2,1,0:T(2,128)S(1)}, f32[8,1,2,512]{3,2,1,0:T(2,128)S(1)}, u32[]{:S(2)}, u32[]{:S(2)}) collective-permute-start(f32[8,1,2,512]{3,2,1,0:T(2,128)S(1)} %get-tuple-element.20), channel_id=1, source_target_pairs={{0,1},{2,3},{4,5},{6,7},{8,9},{10,11},{12,13},{14,15},{16,17},{18,... | collective-permute-start | bytes 98312 | tf_op jit(solution)/shard_map/ppermute | solution.py:16
  31.4 5.8 %collective-permute-start.3 = (f32[8,1,2,512]{3,2,1,0:T(2,128)S(1)}, f32[8,1,2,512]{3,2,1,0:T(2,128)S(1)}, u32[]{:S(2)}, u32[]{:S(2)}) collective-permute-start(f32[8,1,2,512]{3,2,1,0:T(2,128)S(1)} %get-tuple-element.21), channel_id=1, source_target_pairs={{1,0},{3,2},{5,4},{7,6},{9,8},{11,10},{13,12},{15,14},{17,16},{19,... | collective-permute-start | bytes 98312 | tf_op jit(solution)/shard_map/ppermute | solution.py:17
  88.2 5.8 %collective-permute-start.4 = (f32[8,1,2,512]{3,2,1,0:T(2,128)S(1)}, f32[8,1,2,512]{3,2,1,0:T(2,128)S(1)}, u32[]{:S(2)}, u32[]{:S(2)}) collective-permute-start(f32[8,1,2,512]{3,2,1,0:T(2,128)S(1)} %get-tuple-element.18), channel_id=1, source_target_pairs={{0,1},{2,3},{4,5},{6,7},{8,9},{10,11},{12,13},{14,15},{16,17},{18,... | collective-permute-start | bytes 98312 | tf_op jit(solution)/shard_map/ppermute | solution.py:16
  92.4 5.8 %collective-permute-start.5 = (f32[8,1,2,512]{3,2,1,0:T(2,128)S(1)}, f32[8,1,2,512]{3,2,1,0:T(2,128)S(1)}, u32[]{:S(2)}, u32[]{:S(2)}) collective-permute-start(f32[8,1,2,512]{3,2,1,0:T(2,128)S(1)} %get-tuple-element.19), channel_id=1, source_target_pairs={{1,0},{3,2},{5,4},{7,6},{9,8},{11,10},{13,12},{15,14},{17,16},{19,... | collective-permute-start | bytes 98312 | tf_op jit(solution)/shard_map/ppermute | solution.py:17
where the time goes:
time: 145 us; the launch traced here: 144 us
  blocking collectives  79.2 us (55%)
  matrix products  26.7 us (18%)
  starting transfers between devices  17.5 us (12%)
  waiting for transfers between devices  8.73 us (6%)
  between operations  6.85 us (5%)
  other arithmetic  3.86 us (3%)
    psum x2, blocking collectives, two_products(): lax.psum((jnp.sum(vector * vector), jnp.sum(vector * applied)), ('ma', 'f...  79.2 us
    dot_general x3, matrix products, beam_image(): jnp.einsum('mfakl,mfbl->mfabk', beam, field, precision=lax.Precision.HIGH...  23.1 us
    ppermute x3, starting transfers between devices, extended(): before = lax.ppermute(last, axis, up)  13.6 us
    ppermute x3, waiting for transfers between devices, extended(): after = lax.ppermute(leading, axis, down)  8.46 us
    ppermute x3, starting transfers between devices, extended(): after = lax.ppermute(leading, axis, down)  3.88 us
    dot_general x3, matrix products, beam_image(): jnp.einsum('mfakl,mfbk->mfabl', beam, weighted, precision=lax.Precision.H...  3.6 us
  transfers between devices with their start and end apart: 6, of which 4 were waited for; matrix products, arithmetic and copies ran while one was open for 7% of the time, Pallas kernels for 0%

commit v1 on v0

--- a/solution.py
+++ b/solution.py
@@ -37,7 +37,7 @@
 
 
 def two_products(vector, applied):
-    return lax.psum((jnp.sum(vector * vector), jnp.sum(vector * applied)), ("ma", "freq"))
+    return lax.psum(lax.psum((jnp.sum(vector * vector), jnp.sum(vector * applied)), "freq"), "ma")
 
 
 def shards(right_side, start_field, beam, noise, inv_power, smooth):

time: 145 us -> 135 us (0.931)
  blocking collectives: 79.2 us -> 72.3 us
  starting transfers between devices: 17.5 us -> 15.5 us
    psum x2 -> x4, blocking collectives: 79.2 us -> 72.3 us  [the longest x2 61.1 us: two_products(): lax.psum(lax.psum((jnp.sum(vector * vector), jnp.sum(vector * applied)),...]
    ppermute x3, starting transfers between devices: 13.6 us -> 11.6 us  [extended(): before = lax.ppermute(last, axis, up)]
where the time goes in v1:
time: 135 us
  blocking collectives  72.3 us (54%)
  matrix products  26.7 us (20%)
  starting transfers between devices  15.5 us (11%)
  waiting for transfers between devices  8.73 us (6%)
  between operations  6.7 us (5%)
  other arithmetic  3.87 us (3%)
    psum x2, blocking collectives, two_products(): lax.psum(lax.psum((jnp.sum(vector * vector), jnp.sum(vector * applied)),...  61.1 us
    dot_general x3, matrix products, beam_image(): jnp.einsum('mfakl,mfbl->mfabk', beam, field, precision=lax.Precision.HIGH...  23.1 us
    ppermute x3, starting transfers between devices, extended(): before = lax.ppermute(last, axis, up)  11.6 us
    psum x2, blocking collectives, two_products(): lax.psum((jnp.sum(vector * vector), jnp.sum(vector * applied)), 'freq')  11.1 us
    ppermute x3, waiting for transfers between devices, extended(): after = lax.ppermute(leading, axis, down)  8.46 us
    ppermute x3, starting transfers between devices, extended(): after = lax.ppermute(leading, axis, down)  3.88 us
    dot_general x3, matrix products, beam_image(): jnp.einsum('mfakl,mfbk->mfabl', beam, weighted, precision=lax.Precision.H...  3.6 us
  transfers between devices with their start and end apart: 6, of which 4 were waited for; matrix products, arithmetic and copies ran while one was open for 7% of the time, Pallas kernels for 0%

profile of v1, /device:TPU:0, one launch (start us, length us, event | category | flops | bytes accessed | tf_op | source)
XLA Modules:
  0.0 135.0 jit_solution(6279468126549038329)
XLA Ops:
  0.7 0.9 fusion.42
  1.6 4.9 %collective-permute-start = (f32[8,1,2,512]{3,2,1,0:T(2,128)S(1)}, f32[8,1,2,512]{3,2,1,0:T(2,128)S(1)}, u32[]{:S(2)}, u32[]{:S(2)}) collective-permute-start(f32[8,1,2,512]{3,2,1,0:T(2,128)S(1)} %get-tuple-element.26), channel_id=1, source_target_pairs={{0,1},{2,3},{4,5},{6,7},{8,9},{10,11},{12,13},{14,15},{16,17},{18,... | collective-permute-start | bytes 98312 | tf_op jit(solution)/shard_map/ppermute | solution.py:16
  6.5 1.3 collective-permute-start.1
  7.8 8.3 %convolution_bitcast_fusion.1 = f32[8,4,2,2,16]{4,3,2,1,0:T(2,128)S(1)} fusion(f32[8,4,2,16,512]{4,3,2,1,0:T(8,128)S(1)} %copy-done, f32[8,4,2,512]{3,2,1,0:T(2,128)} %param.7), kind=kOutput, calls=%fused_computation.1 | convolution fusion | flops 12582912 | bytes 2236416 | tf_op jit(solution)/shard_map/mfakl,mfbl->mfabk/dot_general | solution.py:23
  16.2 1.1 convolution_bitcast_fusion
  17.6 0.3 fusion.11
  17.9 7.4 %fusion.15 = f32[8,4,2,2,16]{4,2,3,1,0:T(2,128)S(1)} fusion(f32[8,4,2,16,512]{4,3,2,1,0:T(8,128)S(1)} %copy-done, f32[8,4,2,512]{3,2,1,0:T(2,128)S(1)} %fusion.11), kind=kOutput, calls=%fused_computation.28 | convolution fusion | flops 12582912 | bytes 2236416 | tf_op jit(solution)/shard_map/mfakl,mfbl->mfabk/dot_general | solution.py:23
  25.4 1.3 fusion.30
  26.9 4.5 %collective-permute-start.2 = (f32[8,1,2,512]{3,2,1,0:T(2,128)S(1)}, f32[8,1,2,512]{3,2,1,0:T(2,128)S(1)}, u32[]{:S(2)}, u32[]{:S(2)}) collective-permute-start(f32[8,1,2,512]{3,2,1,0:T(2,128)S(1)} %get-tuple-element.24), channel_id=1, source_target_pairs={{0,1},{2,3},{4,5},{6,7},{8,9},{10,11},{12,13},{14,15},{16,17},{18,... | collective-permute-start | bytes 98312 | tf_op jit(solution)/shard_map/ppermute | solution.py:16
  31.4 1.3 collective-permute-start.3
  32.7 0.1 fusion.21
  33.0 4.2 %collective-permute-done.3 = f32[8,1,2,512]{3,2,1,0:T(2,128)S(1)} collective-permute-done((f32[8,1,2,512]{3,2,1,0:T(2,128)S(1)}, f32[8,1,2,512]{3,2,1,0:T(2,128)S(1)}, u32[]{:S(2)}, u32[]{:S(2)}) %collective-permute-start.3) | collective-permute-done | bytes 32800 | tf_op jit(solution)/shard_map/ppermute | solution.py:17
  37.2 1.1 multiply_reduce_fusion.2
  38.3 5.5 %all-reduce.3 = (f32[]{:T(128)}, f32[]{:T(128)}) all-reduce(f32[]{:T(128)} %get-tuple-element.5, f32[]{:T(128)} %get-tuple-element.4), channel_id=1, replica_groups=mesh['ma'=16,'freq'=2] {'freq'}, use_global_device_ids=true, to_apply=%region_1.0 | all-reduce | flops 2 | bytes 16 | tf_op jit(solution)/shard_map/psum | solution.py:40
  43.8 30.9 %all-reduce.1 = (f32[]{:T(128)}, f32[]{:T(128)}) all-reduce(f32[]{:T(128)} %get-tuple-element.12, f32[]{:T(128)} %get-tuple-element.13), channel_id=1, replica_groups=mesh['ma'=16,'freq'=2] {'ma'}, use_global_device_ids=true, to_apply=%region_2.0 | all-reduce | flops 2 | bytes 16 | tf_op jit(solution)/shard_map/psum | solution.py:40
  76.2 7.4 %fusion.13 = f32[8,4,2,2,16]{4,2,3,1,0:T(2,128)S(1)} fusion(f32[8,4,2,16,512]{4,3,2,1,0:T(8,128)S(1)} %copy-done, f32[8,4,2,512]{3,2,1,0:T(2,128)S(1)} %bitcast.90), kind=kOutput, calls=%fused_computation.26 | convolution fusion | flops 12582912 | bytes 2236416 | tf_op jit(solution)/shard_map/mfakl,mfbl->mfabk/dot_general | solution.py:23
  83.6 1.1 fusion.28
  84.9 2.2 %collective-permute-start.4 = (f32[8,1,2,512]{3,2,1,0:T(2,128)S(1)}, f32[8,1,2,512]{3,2,1,0:T(2,128)S(1)}, u32[]{:S(2)}, u32[]{:S(2)}) collective-permute-start(f32[8,1,2,512]{3,2,1,0:T(2,128)S(1)} %get-tuple-element.22), channel_id=1, source_target_pairs={{0,1},{2,3},{4,5},{6,7},{8,9},{10,11},{12,13},{14,15},{16,17},{18,... | collective-permute-start | bytes 98312 | tf_op jit(solution)/shard_map/ppermute | solution.py:16
  87.1 1.3 collective-permute-start.5
  88.7 4.2 %collective-permute-done.5 = f32[8,1,2,512]{3,2,1,0:T(2,128)S(1)} collective-permute-done((f32[8,1,2,512]{3,2,1,0:T(2,128)S(1)}, f32[8,1,2,512]{3,2,1,0:T(2,128)S(1)}, u32[]{:S(2)}, u32[]{:S(2)}) %collective-permute-start.5) | collective-permute-done | bytes 32800 | tf_op jit(solution)/shard_map/ppermute | solution.py:17
  92.9 1.1 multiply_reduce_fusion
  94.1 5.6 %all-reduce.2 = (f32[]{:T(128)}, f32[]{:T(128)}) all-reduce(f32[]{:T(128)} %get-tuple-element.3, f32[]{:T(128)} %get-tuple-element.2), channel_id=1, replica_groups=mesh['ma'=16,'freq'=2] {'freq'}, use_global_device_ids=true, to_apply=%region_7.0 | all-reduce | flops 2 | bytes 16 | tf_op jit(solution)/shard_map/psum | solution.py:40
  99.6 30.2 %all-reduce = (f32[]{:T(128)}, f32[]{:T(128)}) all-reduce(f32[]{:T(128)} %get-tuple-element.10, f32[]{:T(128)} %get-tuple-element.11), channel_id=1, replica_groups=mesh['ma'=16,'freq'=2] {'ma'}, use_global_device_ids=true, to_apply=%region_8.0 | all-reduce | flops 2 | bytes 16 | tf_op jit(solution)/shard_map/psum | solution.py:40
  134.2 0.8 multiply_subtract_fusion
  (34 shorter events, 1.1 us)
Async XLA Ops:
  0.6 7.1 %copy-start = (f32[8,4,2,16,512]{4,3,2,1,0:T(8,128)S(1)}, f32[8,4,2,16,512]{4,3,2,1,0:T(8,128)}, u32[]{:S(2)}) copy-start(f32[8,4,2,16,512]{4,3,2,1,0:T(8,128)} %param.8) | copy-start | bytes 6291460
  0.6 15.5 %copy-start.2 = (f32[8,4,16]{2,1,0:T(4,128)S(1)}, f32[8,4,16]{2,1,0:T(4,128)}, u32[]{:S(2)}) copy-start(f32[8,4,16]{2,1,0:T(4,128)} %param.9) | copy-start | bytes 6148
  1.6 16.0 %collective-permute-start = (f32[8,1,2,512]{3,2,1,0:T(2,128)S(1)}, f32[8,1,2,512]{3,2,1,0:T(2,128)S(1)}, u32[]{:S(2)}, u32[]{:S(2)}) collective-permute-start(f32[8,1,2,512]{3,2,1,0:T(2,128)S(1)} %get-tuple-element.26), channel_id=1, source_target_pairs={{0,1},{2,3},{4,5},{6,7},{8,9},{10,11},{12,13},{14,15},{16,17},{18,... | collective-permute-start | bytes 98312 | tf_op jit(solution)/shard_map/ppermute | solution.py:16
  6.5 11.1 %collective-permute-start.1 = (f32[8,1,2,512]{3,2,1,0:T(2,128)S(1)}, f32[8,1,2,512]{3,2,1,0:T(2,128)S(1)}, u32[]{:S(2)}, u32[]{:S(2)}) collective-permute-start(f32[8,1,2,512]{3,2,1,0:T(2,128)S(1)} %get-tuple-element.27), channel_id=1, source_target_pairs={{1,0},{3,2},{5,4},{7,6},{9,8},{11,10},{13,12},{15,14},{17,16},{19,... | collective-permute-start | bytes 98312 | tf_op jit(solution)/shard_map/ppermute | solution.py:17
  16.1 1.5 %copy-start.1 = (f32[8,4,2,512]{3,2,1,0:T(2,128)S(1)}, f32[8,4,2,512]{3,2,1,0:T(2,128)}, u32[]{:S(2)}) copy-start(f32[8,4,2,512]{3,2,1,0:T(2,128)} %param.7) | copy-start | bytes 393220
  16.1 1.5 %copy-start.3 = (f32[8,4,2,512]{3,2,1,0:T(2,128)S(1)}, f32[8,4,2,512]{3,2,1,0:T(2,128)}, u32[]{:S(2)}) copy-start(f32[8,4,2,512]{3,2,1,0:T(2,128)} %param.6) | copy-start | bytes 393220
  16.1 1.6 %copy-start.4 = (f32[512]{0:T(512)S(1)}, f32[512]{0:T(512)}, u32[]{:S(2)}) copy-start(f32[512]{0:T(512)} %param.11) | copy-start | bytes 6148
  16.1 1.5 %copy-start.5 = (f32[512]{0:T(512)S(1)}, f32[512]{0:T(512)}, u32[]{:S(2)}) copy-start(f32[512]{0:T(512)} %param.10) | copy-start | bytes 6148
  26.9 6.1 %collective-permute-start.2 = (f32[8,1,2,512]{3,2,1,0:T(2,128)S(1)}, f32[8,1,2,512]{3,2,1,0:T(2,128)S(1)}, u32[]{:S(2)}, u32[]{:S(2)}) collective-permute-start(f32[8,1,2,512]{3,2,1,0:T(2,128)S(1)} %get-tuple-element.24), channel_id=1, source_target_pairs={{0,1},{2,3},{4,5},{6,7},{8,9},{10,11},{12,13},{14,15},{16,17},{18,... | collective-permute-start | bytes 98312 | tf_op jit(solution)/shard_map/ppermute | solution.py:16
  31.4 5.8 %collective-permute-start.3 = (f32[8,1,2,512]{3,2,1,0:T(2,128)S(1)}, f32[8,1,2,512]{3,2,1,0:T(2,128)S(1)}, u32[]{:S(2)}, u32[]{:S(2)}) collective-permute-start(f32[8,1,2,512]{3,2,1,0:T(2,128)S(1)} %get-tuple-element.25), channel_id=1, source_target_pairs={{1,0},{3,2},{5,4},{7,6},{9,8},{11,10},{13,12},{15,14},{17,16},{19,... | collective-permute-start | bytes 98312 | tf_op jit(solution)/shard_map/ppermute | solution.py:17
  84.9 3.8 %collective-permute-start.4 = (f32[8,1,2,512]{3,2,1,0:T(2,128)S(1)}, f32[8,1,2,512]{3,2,1,0:T(2,128)S(1)}, u32[]{:S(2)}, u32[]{:S(2)}) collective-permute-start(f32[8,1,2,512]{3,2,1,0:T(2,128)S(1)} %get-tuple-element.22), channel_id=1, source_target_pairs={{0,1},{2,3},{4,5},{6,7},{8,9},{10,11},{12,13},{14,15},{16,17},{18,... | collective-permute-start | bytes 98312 | tf_op jit(solution)/shard_map/ppermute | solution.py:16
  87.1 5.8 %collective-permute-start.5 = (f32[8,1,2,512]{3,2,1,0:T(2,128)S(1)}, f32[8,1,2,512]{3,2,1,0:T(2,128)S(1)}, u32[]{:S(2)}, u32[]{:S(2)}) collective-permute-start(f32[8,1,2,512]{3,2,1,0:T(2,128)S(1)} %get-tuple-element.23), channel_id=1, source_target_pairs={{1,0},{3,2},{5,4},{7,6},{9,8},{11,10},{13,12},{15,14},{17,16},{19,... | collective-permute-start | bytes 98312 | tf_op jit(solution)/shard_map/ppermute | solution.py:17
